TPU v7x, 32 devices: a whole 2x2x4 slice. The times are simulated.
32 devices in a mesh: group: 4 (over z), member: 8 (over y, x, core).
Axes of the slice: x: 2, y: 2, z: 4, core: 2. Of those that a mesh axis runs over, the one named last changes fastest.
Arguments:
- source: bfloat16 [32768, 256], P(('group', 'member')), may hold values from -6 to 6
- target: bfloat16 [8192, 256], P(('group', 'member')), may hold values from -6 to 6
- pair_source: int32 [32, 32], P(('group', 'member')), may hold values from 0 to 3, as said below
- pair_target: int32 [32, 32], P(('group', 'member')), may hold values from 0 to 15, as said below
- pair_count: int32 [32], P(('group', 'member')), may hold values from 4 to 32, as said below
Outputs:
- log_source: float32 [32768], P(('group', 'member'))
- log_target: float32 [8192], P(('group', 'member'))
Inputs may be any that keep to these rules, and one draw needn't show every extreme that they name: `pair_source`: each entry is the device's own source tile, 0 to 3; slots 0 to 3 name each of them once, and no (source tile, window tile) pair stands twice on one device. `pair_target`: window index of the pair's target tile; on every device slot 0 names the device's own target tile (index equal to its member index). `pair_count`: at least 4; in every group one device has exactly 32.
All inputs are finite; a program needn't handle non-finite values.
Results may differ from a plain program's by a relative error of at most 0.0031.
Values may be sent and summed in bfloat16 or wider, within the bound.
No kernel may reach another device: no remote copies, remote signals or barrier semaphores. Data moves between devices by JAX's collectives and lax.ppermute only.
A program may use at most 128 MiB of HBM per device.

v0:
```python
import math
import jax
import jax.numpy as jnp
from jax import lax
from jax.sharding import PartitionSpec as P

ITERS = 2
regularizer_strength = 0.05


def shifted(x, axis, by):
    length = lax.axis_size(axis)
    return lax.ppermute(x, axis, [(i, (i + by) % length) for i in range(length)])


def normalize(values):
    floats = values.astype(jnp.float32)
    return (floats / jnp.sqrt(jnp.sum(floats * floats, axis=1, keepdims=True) + 1e-06)).astype(
        jnp.bfloat16
    )


def shards(source, target, pair_source, pair_target, pair_count):
    constituent_entries = lax.axis_size("member")
    cells_per_tile = target.shape[0]
    latent_width = target.shape[1]
    tiles_here = source.shape[0] // cells_per_tile
    unit_source = normalize(source).reshape(tiles_here, cells_per_tile, latent_width)
    unit_target = normalize(target)
    next_target = shifted(unit_target, "group", -1)
    own_window, next_window = (
        lax.all_gather(unit_target, "member", axis=0, tiled=True),
        lax.all_gather(next_target, "member", axis=0, tiled=True),
    )
    window = jnp.concatenate([own_window, next_window], 0).reshape(
        2 * constituent_entries, cells_per_tile, latent_width
    )
    slot_count = pair_source.shape[1]
    block_size = math.gcd(slot_count, 16)
    block_count = slot_count // block_size
    source_slots = pair_source[0]
    window_slots = pair_target[0]
    surviving_indicator = (jnp.arange(slot_count, dtype=jnp.int32) < pair_count[0]).astype(
        jnp.float32
    )
    block_ids = jnp.arange(block_count, dtype=jnp.int32)
    source_blocks = source_slots.reshape(block_count, block_size)
    window_blocks = window_slots.reshape(block_count, block_size)
    keep_blocks = surviving_indicator.reshape(block_count, block_size)
    pick_source = (
        source_slots[:, None] == jnp.arange(tiles_here, dtype=jnp.int32)[None, :]
    ).astype(jnp.float32)
    pick_window = (
        window_slots[:, None] == jnp.arange(2 * constituent_entries, dtype=jnp.int32)[None, :]
    ).astype(jnp.float32)

    def kernels(block_items):
        source_ids, frame_labels, retained_portion = block_items
        own_rows = unit_source[source_ids]
        partners = window[frame_labels]
        similarity_logits = jnp.einsum(
            "pid,pjd->pij", own_rows, partners, preferred_element_type=jnp.float32
        )
        return (
            jnp.exp(similarity_logits / regularizer_strength)
            / cells_per_tile
            * retained_portion[:, None, None]
        ).astype(jnp.bfloat16)

    cached = lax.map(kernels, (source_blocks, window_blocks, keep_blocks))

    def kernel_block(block_items):
        block_index, source_ids, frame_labels, retained_portion = block_items
        return lax.dynamic_index_in_dim(cached, block_index, 0, keepdims=False)

    scale_window = jnp.ones((2 * constituent_entries, cells_per_tile), jnp.float32)
    scale_source = jnp.ones((tiles_here, cells_per_tile), jnp.float32)
    scale_target = jnp.ones((cells_per_tile,), jnp.float32)
    block_inputs = (block_ids, source_blocks, window_blocks, keep_blocks)
    for sweep_number in range(ITERS):

        def row_block(block_items, scale_window=scale_window):
            boltzmann_factor_patches = kernel_block(block_items)
            weights = scale_window[block_items[2]]
            return jnp.sum(
                boltzmann_factor_patches.astype(jnp.float32) * weights[:, None, :], axis=2
            )

        row_parts = lax.map(row_block, block_inputs).reshape(slot_count, cells_per_tile)
        row_sums = jnp.einsum("ps,pi->si", pick_source, row_parts, precision=lax.Precision.HIGHEST)
        scale_source = 1.0 / row_sums

        def column_block(block_items, scale_source=scale_source):
            boltzmann_factor_patches = kernel_block(block_items)
            weights = scale_source[block_items[1]]
            return jnp.sum(
                boltzmann_factor_patches.astype(jnp.float32) * weights[:, :, None], axis=1
            )

        column_parts = lax.map(column_block, block_inputs).reshape(slot_count, cells_per_tile)
        column_terms = jnp.einsum(
            "pw,pj->wj", pick_window, column_parts, precision=lax.Precision.HIGHEST
        )
        arrived_next = shifted(column_terms[constituent_entries:], "group", 1)
        columns = lax.psum_scatter(
            column_terms[:constituent_entries] + arrived_next,
            "member",
            scatter_dimension=0,
            tiled=True,
        )[0]
        scale_target = float(tiles_here) / columns
        if sweep_number + 1 < ITERS:
            neighbour_scale = shifted(scale_target[None], "group", -1)
            range_scale, next_scale = (
                lax.all_gather(scale_target[None], "member", axis=0, tiled=True),
                lax.all_gather(neighbour_scale, "member", axis=0, tiled=True),
            )
            scale_window = jnp.concatenate([range_scale, next_scale], 0)
    return (jnp.log(scale_source).reshape(tiles_here * cells_per_tile), jnp.log(scale_target))


def solution(mesh):
    placed = (
        P(("group", "member"), None),
        P(("group", "member"), None),
        P(("group", "member"), None),
        P(("group", "member"), None),
        P(("group", "member")),
    )
    return jax.shard_map(
        shards,
        mesh=mesh,
        in_specs=placed,
        out_specs=(P(("group", "member")), P(("group", "member"))),
        check_vma=False,
    )
```

profile of v0, /device:TPU:0, one launch (start us, length us, event | category | flops | bytes accessed | tf_op | source)
XLA Modules:
  0.0 186.2 jit_solution(13188330610118061224)
XLA Ops:
  7.2 1.0 fusion.20
  8.2 1.7 fusion.21
  10.0 5.1 %collective-permute-start = (bf16[256,256]{1,0:T(8,128)(2,1)}, bf16[256,256]{1,0:T(8,128)(2,1)S(1)}, u32[]{:S(2)}, u32[]{:S(2)}) collective-permute-start(bf16[256,256]{1,0:T(8,128)(2,1)} %fusion.21), channel_id=1, source_target_pairs={{0,24},{8,0},{16,8},{24,16},{1,25},{9,1},{17,9},{25,17},{2,26},{10... | collective-permute-start | bytes 393224 | tf_op jit(solution)/shard_map/ppermute | solution.py:13
  15.1 3.1 %collective-permute-done = bf16[256,256]{1,0:T(8,128)(2,1)S(1)} collective-permute-done((bf16[256,256]{1,0:T(8,128)(2,1)}, bf16[256,256]{1,0:T(8,128)(2,1)S(1)}, u32[]{:S(2)}, u32[]{:S(2)}) %collective-permute-start) | collective-permute-done | bytes 131104 | tf_op jit(solution)/shard_map/ppermute | solution.py:13
  18.2 0.6 copy-done
  18.9 0.5 broadcast.208
  19.4 1.3 reduce.6
  20.8 1.3 reduce.7
  22.8 1.3 fusion.18
  24.1 1.2 fusion.19
  25.4 10.8 %all-gather.5.cloned.1.call-done = bf16[2048,256]{1,0:T(8,128)(2,1)} async-done(((bf16[256,256]{1,0:T(8,128)(2,1)}), bf16[2048,256]{1,0:T(8,128)(2,1)}) %all-gather.5.cloned.1.call-update) | async-done | bytes 1048592 | tf_op jit(solution)/shard_map/all_gather | solution.py:32
  36.2 25.3 %all-gather.7.cloned.1.call-done = bf16[2048,256]{1,0:T(8,128)(2,1)} async-done(((bf16[256,256]{1,0:T(8,128)(2,1)}), bf16[2048,256]{1,0:T(8,128)(2,1)}) %all-gather.7.cloned.1.call-update) | async-done | bytes 1048592 | tf_op jit(solution)/shard_map/all_gather | solution.py:33
  61.5 1.7 pad_maximum_fusion
  63.1 16.9 %while.50 = (s32[]{:T(128)}, bf16[2,16,256,256]{3,2,1,0:T(8,128)(2,1)}, s32[2,16]{1,0:T(2,128)S(1)}, bf16[4,256,256]{2,1,0:T(8,128)(2,1)S(1)}, s32[2,16]{1,0:T(2...) while((s32[]{:T(128)}, bf16[2,16,256,256]{3,2,1,0:T(8,128)(2,1)}, ...), condition=%wide.region_3.4_spmd, body=%wide.region_2.3_spmd.sunk | while | flops 540018816 | bytes 14689565 | solution.py:70
  63.2 2.0 %gather_fusion = bf16[16,256,256]{2,1,0:T(8,128)(2,1)} fusion(bf16[4,256,256]{2,1,0:T(8,128)(2,1)S(1)} %get-tuple-element.437, s32[1024]{0:T(1024)S(1)} %pad_clamp_fusion.12), kind=kCustom, calls=%fused_computation.clone.1 | custom fusion | bytes 4194368 | tf_op jit(solution)/shard_map/while/body/eval_jaxpr/gather | solution.py:59
  65.2 2.0 %gather_fusion.1 = bf16[16,256,256]{2,1,0:T(8,128)(2,1)} fusion(bf16[16,256,256]{2,1,0:T(8,128)(2,1)S(1)} %get-tuple-element.439, s32[1024]{0:T(1024)S(1)} %pad_clamp_fusion.13), kind=kCustom, calls=%fused_computation.1.clone.1 | custom fusion | bytes 4194368 | tf_op jit(solution)/shard_map/while/body/eval_jaxpr/gather | solution.py:60
  67.2 4.4 %bitcast_dynamic-update-slice_fusion.10 = bf16[2,16,256,256]{3,2,1,0:T(8,128)(2,1)} fusion(bf16[2,16,256,256]{3,2,1,0:T(8,128)(2,1)} %get-tuple-element.427, s32[]{:T(128)} %get-tuple-element.426, f32[16]{0:T(128)S(1)} %fusion.50, bf16[16,256,256]{2,1,0:T(8,128)(2,1)} %gather_fusion, bf16[16,256,256]{2,1,0:T(8,128)(2,1)} %gather_fusion.1), kind=kOutput, calls=%fused_computation.7.clone.1 | convolution fusion | flops 540016640 | bytes 6292032 | tf_op jit(solution)/shard_map/while/body/eval_jaxpr/pid,pjd->pij/dot_general | solution.py:61
  71.7 2.0 %gather_fusion = bf16[16,256,256]{2,1,0:T(8,128)(2,1)} fusion(bf16[4,256,256]{2,1,0:T(8,128)(2,1)S(1)} %get-tuple-element.437, s32[1024]{0:T(1024)S(1)} %pad_clamp_fusion.12), kind=kCustom, calls=%fused_computation.clone.1 | custom fusion | bytes 4194368 | tf_op jit(solution)/shard_map/while/body/eval_jaxpr/gather | solution.py:59
  73.7 2.0 %gather_fusion.1 = bf16[16,256,256]{2,1,0:T(8,128)(2,1)} fusion(bf16[16,256,256]{2,1,0:T(8,128)(2,1)S(1)} %get-tuple-element.439, s32[1024]{0:T(1024)S(1)} %pad_clamp_fusion.13), kind=kCustom, calls=%fused_computation.1.clone.1 | custom fusion | bytes 4194368 | tf_op jit(solution)/shard_map/while/body/eval_jaxpr/gather | solution.py:60
  75.7 4.3 %bitcast_dynamic-update-slice_fusion.10 = bf16[2,16,256,256]{3,2,1,0:T(8,128)(2,1)} fusion(bf16[2,16,256,256]{3,2,1,0:T(8,128)(2,1)} %get-tuple-element.427, s32[]{:T(128)} %get-tuple-element.426, f32[16]{0:T(128)S(1)} %fusion.50, bf16[16,256,256]{2,1,0:T(8,128)(2,1)} %gather_fusion, bf16[16,256,256]{2,1,0:T(8,128)(2,1)} %gather_fusion.1), kind=kOutput, calls=%fused_computation.7.clone.1 | convolution fusion | flops 540016640 | bytes 6292032 | tf_op jit(solution)/shard_map/while/body/eval_jaxpr/pid,pjd->pij/dot_general | solution.py:61
  80.1 10.6 %while.51 = (s32[]{:T(128)}, f32[2,16,256]{2,1,0:T(8,128)S(1)}, s32[2]{0:T(128)S(1)}, bf16[2,16,256,256]{3,2,1,0:T(8,128)(2,1)}, s32[2,16]{1,0:T(2,128)S(1)}, /*index=5*/s32[]{:T(128)}, f32[]{:T(128)}, s32[]{:T(128)}, s32[]{:T(128)}) while((s32[]{:T(128)}, f32[2,16,256]{2,1,0:T(8,128)S(1)}, s32[2]{0:T(128)S(1)}, ...), condition=%wide.region_6.7_spmd, body=%wide.region_4.6_spmd.sunk | while | flops 3142709 | bytes 2216347 | solution.py:89
  80.1 0.6 dynamic_slice.118
  82.6 0.6 gather_fusion.2
  83.2 2.2 %fusion.53 = f32[16,256]{1,0:T(8,128)S(1)} fusion(f32[16,256]{1,0:T(8,128)S(1)} %gather_fusion.2, bf16[2,16,256,256]{3,2,1,0:T(8,128)(2,1)} %get-tuple-element.463, s32[]{:T(128)S(6)} %select_n.102), kind=kLoop, calls=%fused_computation.22.clone.1 | loop fusion | flops 3141632 | bytes 2129924 | tf_op jit(solution)/shard_map/while/body/eval_jaxpr/reduce_sum | solution.py:85
  85.4 0.6 dynamic_slice.118
  87.9 0.6 gather_fusion.2
  88.5 2.2 %fusion.53 = f32[16,256]{1,0:T(8,128)S(1)} fusion(f32[16,256]{1,0:T(8,128)S(1)} %gather_fusion.2, bf16[2,16,256,256]{3,2,1,0:T(8,128)(2,1)} %get-tuple-element.463, s32[]{:T(128)S(6)} %select_n.102), kind=kLoop, calls=%fused_computation.22.clone.1 | loop fusion | flops 3141632 | bytes 2129924 | tf_op jit(solution)/shard_map/while/body/eval_jaxpr/reduce_sum | solution.py:85
  91.0 10.3 %while.52 = (s32[]{:T(128)}, f32[2,16,256]{2,1,0:T(8,128)S(1)}, s32[2]{0:T(128)S(1)}, bf16[2,16,256,256]{3,2,1,0:T(8,128)(2,1)}, s32[2,16]{1,0:T(2,128)S(1)}, /*...) while((s32[]{:T(128)}, f32[2,16,256]{2,1,0:T(8,128)S(1)}, s32[2]{0:T(128)S(1)}, ...), condition=%wide.region_9.10_spmd, body=%wide.region_7.9_spmd.sunk | while | flops 3142709 | bytes 2199959 | solution.py:100
  91.0 0.6 dynamic_slice.121
  93.6 0.6 gather_fusion.3
  94.2 1.9 %fusion.55 = f32[16,256]{1,0:T(8,128)S(1)} fusion(f32[16,256]{1,0:T(8,128)S(1)} %gather_fusion.3, bf16[2,16,256,256]{3,2,1,0:T(8,128)(2,1)} %get-tuple-element.490, s32[]{:T(128)S(6)} %select_n.104), kind=kLoop, calls=%fused_computation.30.clone.1 | loop fusion | flops 3141632 | bytes 2129924 | tf_op jit(solution)/shard_map/while/body/eval_jaxpr/reduce_sum | solution.py:96
  96.2 0.6 dynamic_slice.121
  98.7 0.6 gather_fusion.3
  99.3 1.9 %fusion.55 = f32[16,256]{1,0:T(8,128)S(1)} fusion(f32[16,256]{1,0:T(8,128)S(1)} %gather_fusion.3, bf16[2,16,256,256]{3,2,1,0:T(8,128)(2,1)} %get-tuple-element.490, s32[]{:T(128)S(6)} %select_n.104), kind=kLoop, calls=%fused_computation.30.clone.1 | loop fusion | flops 3141632 | bytes 2129924 | tf_op jit(solution)/shard_map/while/body/eval_jaxpr/reduce_sum | solution.py:96
  101.3 0.3 fusion.23
  101.6 1.5 collective-permute-start.1
  103.1 0.6 dynamic-slice
  103.7 3.4 %collective-permute-done.1 = f32[8,256]{1,0:T(8,128)S(1)} collective-permute-done((f32[8,256]{1,0:T(8,128)S(1)}, f32[8,256]{1,0:T(8,128)S(1)}, u32[]{:S(2)}, u32[]{:S(2)}) %collective-permute-start.1) | collective-permute-done | bytes 8224 | tf_op jit(solution)/shard_map/ppermute | solution.py:13
  107.1 12.2 %all-reduce = f32[8,256]{1,0:T(8,128)S(1)} all-reduce(f32[8,256]{1,0:T(8,128)S(1)} %slice_add_fusion.1), channel_id=2, replica_groups=mesh['group'=4,'member'=8] {'member'}, use_global_device_ids=true, to_apply=%region_10.11.clone | all-reduce | flops 2048 | bytes 16384
  119.3 0.6 dynamic-slice_divide_fusion.1
  119.9 0.6 fusion.35
  120.5 1.6 collective-permute-start.2
  122.1 8.9 %all-gather = f32[8,1,256]{2,1,0:T(1,128)S(1)} all-gather(f32[1,1,256]{2,1,0:T(1,128)S(1)} %fusion.35), channel_id=1, replica_groups=mesh['group'=4,'member'=8] {'member'}, dimensions={0}, use_global_device_ids=true | all-gather | bytes 9216 | tf_op jit(solution)/shard_map/all_gather | solution.py:115
  131.0 8.0 %all-gather.1 = f32[8,1,256]{2,1,0:T(1,128)S(1)} all-gather(f32[1,1,256]{2,1,0:T(1,128)S(1)} %bitcast.167), channel_id=1, replica_groups=mesh['group'=4,'member'=8] {'member'}, dimensions={0}, use_global_device_ids=true | all-gather | bytes 9216 | tf_op jit(solution)/shard_map/all_gather | solution.py:116
  139.0 10.6 %while.53 = (s32[]{:T(128)}, f32[2,16,256]{2,1,0:T(8,128)S(1)}, s32[2]{0:T(128)S(1)}, bf16[2,16,256,256]{3,2,1,0:T(8,128)(2,1)}, s32[2,16]{1,0:T(2,128)S(1)}, /*...) while((s32[]{:T(128)}, f32[2,16,256]{2,1,0:T(8,128)S(1)}, s32[2]{0:T(128)S(1)}, ...), condition=%wide.region_13.14_spmd, body=%wide.region_11.13_spmd.sunk | while | flops 3142709 | bytes 2199959 | solution.py:89
  139.0 0.6 dynamic_slice.124
  141.4 0.6 gather_fusion.4
  142.0 2.2 %fusion.57 = f32[16,256]{1,0:T(8,128)S(1)} fusion(f32[16,256]{1,0:T(8,128)S(1)} %gather_fusion.4, bf16[2,16,256,256]{3,2,1,0:T(8,128)(2,1)} %get-tuple-element.517, s32[]{:T(128)S(6)} %select_n.106), kind=kLoop, calls=%fused_computation.38.clone.1 | loop fusion | flops 3141632 | bytes 2129924 | tf_op jit(solution)/shard_map/while/body/eval_jaxpr/reduce_sum | solution.py:85
  144.3 0.6 dynamic_slice.124
  146.7 0.6 gather_fusion.4
  147.3 2.2 %fusion.57 = f32[16,256]{1,0:T(8,128)S(1)} fusion(f32[16,256]{1,0:T(8,128)S(1)} %gather_fusion.4, bf16[2,16,256,256]{3,2,1,0:T(8,128)(2,1)} %get-tuple-element.517, s32[]{:T(128)S(6)} %select_n.106), kind=kLoop, calls=%fused_computation.38.clone.1 | loop fusion | flops 3141632 | bytes 2129924 | tf_op jit(solution)/shard_map/while/body/eval_jaxpr/reduce_sum | solution.py:85
  149.8 10.3 %while.54 = (s32[]{:T(128)}, f32[2,16,256]{2,1,0:T(8,128)S(1)}, s32[2]{0:T(128)S(1)}, bf16[2,16,256,256]{3,2,1,0:T(8,128)(2,1)}, s32[2,16]{1,0:T(2,128)S(1)}, /*...) while((s32[]{:T(128)}, f32[2,16,256]{2,1,0:T(8,128)S(1)}, s32[2]{0:T(128)S(1)}, ...), condition=%wide.region_16.17_spmd, body=%wide.region_14.16_spmd.sunk | while | flops 3142709 | bytes 2199959 | solution.py:100
  149.9 0.6 dynamic_slice.127
  152.4 0.6 gather_fusion.5
  153.0 1.9 %fusion.59 = f32[16,256]{1,0:T(8,128)S(1)} fusion(f32[16,256]{1,0:T(8,128)S(1)} %gather_fusion.5, bf16[2,16,256,256]{3,2,1,0:T(8,128)(2,1)} %get-tuple-element.544, s32[]{:T(128)S(6)} %select_n.108), kind=kLoop, calls=%fused_computation.46.clone.1 | loop fusion | flops 3141632 | bytes 2129924 | tf_op jit(solution)/shard_map/while/body/eval_jaxpr/reduce_sum | solution.py:96
  155.0 0.6 dynamic_slice.127
  157.5 0.6 gather_fusion.5
  158.1 1.9 %fusion.59 = f32[16,256]{1,0:T(8,128)S(1)} fusion(f32[16,256]{1,0:T(8,128)S(1)} %gather_fusion.5, bf16[2,16,256,256]{3,2,1,0:T(8,128)(2,1)} %get-tuple-element.544, s32[]{:T(128)S(6)} %select_n.108), kind=kLoop, calls=%fused_computation.46.clone.1 | loop fusion | flops 3141632 | bytes 2129924 | tf_op jit(solution)/shard_map/while/body/eval_jaxpr/reduce_sum | solution.py:96
  160.1 0.3 fusion.22
  160.4 0.5 collective-permute-start.3
  160.9 0.6 copy.9
  161.5 4.3 %collective-permute-done.3 = f32[8,256]{1,0:T(8,128)S(1)} collective-permute-done((f32[8,256]{1,0:T(8,128)S(1)}, f32[8,256]{1,0:T(8,128)S(1)}, u32[]{:S(2)}, u32[]{:S(2)}) %collective-permute-start.3) | collective-permute-done | bytes 8224 | tf_op jit(solution)/shard_map/ppermute | solution.py:13
  165.9 12.3 %all-reduce.1 = f32[8,256]{1,0:T(8,128)S(1)} all-reduce(f32[8,256]{1,0:T(8,128)S(1)} %slice_add_fusion), channel_id=3, replica_groups=mesh['group'=4,'member'=8] {'member'}, use_global_device_ids=true, to_apply=%region_17.18.clone | all-reduce | flops 2048 | bytes 16384
  178.2 1.2 fusion.28
  (70 shorter events, 1.2 us)
Async XLA Ops:
  7.2 29.0 %all-gather.5.cloned.1.call-start = ((), (), s32[]{:S(2)}) async-start(), calls=%async_computation | async-start | bytes 1179648 | tf_op jit(solution)/shard_map/all_gather | solution.py:32
  9.9 51.5 %all-gather.7.cloned.1.call-start = ((), (), s32[]{:S(2)}) async-start(), calls=%async_computation.1 | async-start | bytes 1179648 | tf_op jit(solution)/shard_map/all_gather | solution.py:33
  10.0 8.2 %collective-permute-start = (bf16[256,256]{1,0:T(8,128)(2,1)}, bf16[256,256]{1,0:T(8,128)(2,1)S(1)}, u32[]{:S(2)}, u32[]{:S(2)}) collective-permute-start(bf16[256,256]{1,0:T(8,128)(2,1)} %fusion.21), channel_id=1, source_target_pairs={{0,24},{8,0},{16,8},{24,16},{1,25},{9,1},{17,9},{25,17},{2,26},{10... | collective-permute-start | bytes 393224 | tf_op jit(solution)/shard_map/ppermute | solution.py:13
  18.2 0.7 copy-start
  80.1 10.7 %copy-start.1 = (s32[1,32]{1,0:T(1,128)S(1)}, s32[1,32]{1,0:T(1,128)}, u32[]{:S(2)}) copy-start(s32[1,32]{1,0:T(1,128)} %param.17) | copy-start | bytes 388
  91.0 10.3 %copy-start.2 = (s32[1,32]{1,0:T(1,128)S(1)}, s32[1,32]{1,0:T(1,128)}, u32[]{:S(2)}) copy-start(s32[1,32]{1,0:T(1,128)} %param.18) | copy-start | bytes 388
  91.0 12.1 %copy-start.3 = (u32[32]{0:T(128)S(1)}, u32[32]{0:T(128)}, u32[]{:S(2)}) copy-start(u32[32]{0:T(128)} %constant.109) | copy-start | bytes 388
  101.6 5.5 %collective-permute-start.1 = (f32[8,256]{1,0:T(8,128)S(1)}, f32[8,256]{1,0:T(8,128)S(1)}, u32[]{:S(2)}, u32[]{:S(2)}) collective-permute-start(f32[8,256]{1,0:T(8,128)S(1)} %slice.29), channel_id=1, source_target_pairs={{0,8},{8,16},{16,24},{24,0},{1,9},{9,17},{17,25},{25,1},{2,10},{10... | collective-permute-start | bytes 24584 | tf_op jit(solution)/shard_map/ppermute | solution.py:13
  120.5 10.5 %collective-permute-start.2 = (f32[1,256]{1,0:T(1,128)S(1)}, f32[1,256]{1,0:T(1,128)S(1)}, u32[]{:S(2)}, u32[]{:S(2)}) collective-permute-start(f32[1,256]{1,0:T(1,128)S(1)} %dynamic-slice_divide_fusion.1), channel_id=1, source_target_pairs={{0,24},{8,0},{16,8},{24,16},{1,25},{9,1},{17,9},{25,17},{2,26},{10... | collective-permute-start | bytes 3080 | tf_op jit(solution)/shard_map/ppermute | solution.py:13
  160.4 5.5 %collective-permute-start.3 = (f32[8,256]{1,0:T(8,128)S(1)}, f32[8,256]{1,0:T(8,128)S(1)}, u32[]{:S(2)}, u32[]{:S(2)}) collective-permute-start(f32[8,256]{1,0:T(8,128)S(1)} %slice.31), channel_id=1, source_target_pairs={{0,8},{8,16},{16,24},{24,0},{1,9},{9,17},{17,25},{25,1},{2,10},{10... | collective-permute-start | bytes 24584 | tf_op jit(solution)/shard_map/ppermute | solution.py:13
Sparse Core Ops, SparseCore 0:
  10.0 26.0 all-gather.4
  38.1 23.3 all-gather.6
where the time goes:
time: 187 us; the launch traced here: 186 us
  waiting for transfers between devices  46.9 us (25%)
  blocking collectives  41.3 us (22%)
  other arithmetic  28.8 us (15%)
  local copies, waits for them, and re-layouts  20.1 us (11%)
  loops' own time  15.6 us (8%)
  between operations  14.9 us (8%)
  matrix products  9.78 us (5%)
  starting transfers between devices  8.88 us (5%)
    all_gather x1, waiting for transfers between devices, shards(): lax.all_gather(next_target, 'member', axis=0, tiled=True)  25.3 us
    unnamed x2, blocking collectives  24.5 us
    all_gather x1, waiting for transfers between devices, shards(): lax.all_gather(unit_target, 'member', axis=0, tiled=True)  10.8 us
    ppermute x4, waiting for transfers between devices, shifted(): lax.ppermute(x, axis, [(i, (i + by) % length) for i in range(length)])  10.8 us
    all_gather x1, blocking collectives, shards(): lax.all_gather(scale_target[None], 'member', axis=0, tiled=True)  8.88 us
    reduce_sum x4, other arithmetic, row_block(): jnp.sum(boltzmann_factor_patches.astype(jnp.float32) * weights[:, None, :...  8.85 us
    ppermute x4, starting transfers between devices, shifted(): lax.ppermute(x, axis, [(i, (i + by) % length) for i in range(length)])  8.8 us
    dot_general x2, matrix products, kernels(): jnp.einsum('pid,pjd->pij', own_rows, partners, preferred_element_type=jnp...  8.75 us
  transfers between devices with their start and end apart: 6, of which 5 were waited for; matrix products, arithmetic and copies ran while one was open for 4% of the time, Pallas kernels for 0%

commit v1 on v0

--- a/solution.py
+++ b/solution.py
@@ -6,6 +6,18 @@
 
 ITERS = 2
 regularizer_strength = 0.05
+
+
+def doubled_up(shard, axis, dim):
+    ways, here, turn = (lax.axis_size(axis), lax.axis_index(axis), shard.shape[dim])
+    line, have = (shard, 1)
+    while have < ways:
+        line = jnp.concatenate(
+            [line, lax.ppermute(line, axis, [(d, (d - have) % ways) for d in range(ways)])],
+            axis=dim,
+        )
+        have = 2 * have
+    return jnp.roll(line, here * turn, axis=dim)
 
 
 def shifted(x, axis, by):
@@ -30,7 +42,7 @@
     next_target = shifted(unit_target, "group", -1)
     own_window, next_window = (
         lax.all_gather(unit_target, "member", axis=0, tiled=True),
-        lax.all_gather(next_target, "member", axis=0, tiled=True),
+        doubled_up(next_target, "member", 0),
     )
     window = jnp.concatenate([own_window, next_window], 0).reshape(
         2 * constituent_entries, cells_per_tile, latent_width

time: 187 us -> 176 us (0.941)
  waiting for transfers between devices: 46.9 us -> 35.8 us
  other arithmetic: 28.8 us -> 25.9 us
    all_gather x1 -> x0, waiting for transfers between devices: 25.3 us -> none  [shards(): lax.all_gather(next_target, 'member', axis=0, tiled=True)]
    ppermute x0 -> x3, waiting for transfers between devices: none -> 23.1 us  [doubled_up(): lax.ppermute(line, axis, [(d, (d - have) % ways) for d in range(ways)])]
    all_gather x1, waiting for transfers between devices: 10.8 us -> 0.01 us  [shards(): lax.all_gather(unit_target, 'member', axis=0, tiled=True)]
    ppermute x0 -> x3, starting transfers between devices: none -> 2.57 us  [doubled_up(): lax.ppermute(line, axis, [(d, (d - have) % ways) for d in range(ways)])]
    ppermute x4, waiting for transfers between devices: 10.8 us -> 12.8 us  [shifted(): lax.ppermute(x, axis, [(i, (i + by) % length) for i in range(length)])]
  transfers between devices with their start and end apart: 6 -> 8, of which waited for: 5 -> 6; matrix products, arithmetic and copies ran while one was open for 4% -> 3% of each run, Pallas kernels for 0% -> 0%
where the time goes in v1:
time: 176 us; the launch traced here: 175 us
  blocking collectives  42.7 us (24%)
  waiting for transfers between devices  35.8 us (20%)
  other arithmetic  25.9 us (15%)
  local copies, waits for them, and re-layouts  20.7 us (12%)
  loops' own time  15.6 us (9%)
  between operations  15 us (9%)
  starting transfers between devices  9.93 us (6%)
  matrix products  9.78 us (6%)
    unnamed x2, blocking collectives  25.8 us
    ppermute x3, waiting for transfers between devices, doubled_up(): lax.ppermute(line, axis, [(d, (d - have) % ways) for d in range(ways)])  23.1 us
    ppermute x4, waiting for transfers between devices, shifted(): lax.ppermute(x, axis, [(i, (i + by) % length) for i in range(length)])  12.8 us
    all_gather x1, blocking collectives, shards(): lax.all_gather(neighbour_scale, 'member', axis=0, tiled=True)  8.98 us
    reduce_sum x4, other arithmetic, row_block(): jnp.sum(boltzmann_factor_patches.astype(jnp.float32) * weights[:, None, :...  8.85 us
    dot_general x2, matrix products, kernels(): jnp.einsum('pid,pjd->pij', own_rows, partners, preferred_element_type=jnp...  8.75 us
    another operation x2, loops' own time, shards(): lax.map(column_block, block_inputs).reshape(slot_count, cells_per_tile)  7.97 us
    all_gather x1, blocking collectives, shards(): lax.all_gather(scale_target[None], 'member', axis=0, tiled=True)  7.86 us
  transfers between devices with their start and end apart: 8, of which 6 were waited for; matrix products, arithmetic and copies ran while one was open for 3% of the time, Pallas kernels for 0%

profile of v1, /device:TPU:0, one launch (start us, length us, event | category | flops | bytes accessed | tf_op | source)
XLA Modules:
  0.0 175.4 jit_solution(1192940600028745861)
XLA Ops:
  7.2 1.1 fusion.20
  8.3 1.0 fusion.21
  9.3 5.1 %collective-permute-start = (bf16[256,256]{1,0:T(8,128)(2,1)S(1)}, bf16[256,256]{1,0:T(8,128)(2,1)S(1)}, u32[]{:S(2)}, u32[]{:S(2)}) collective-permute-start(bf16[256,256]{1,0:T(8,128)(2,1)S(1)} %fusion.21), channel_id=1, source_target_pairs={{0,24},{8,0},{16,8},{24,16},{1,25},{9,1},{17,9},{25,17},{2,26},{10... | collective-permute-start | bytes 393224 | tf_op jit(solution)/shard_map/ppermute | solution.py:25
  14.5 2.8 %collective-permute-done = bf16[256,256]{1,0:T(8,128)(2,1)S(1)} collective-permute-done((bf16[256,256]{1,0:T(8,128)(2,1)S(1)}, bf16[256,256]{1,0:T(8,128)(2,1)S(1)}, u32[]{:S(2)}, u32[]{:S(2)}) %collective-permute-start) | collective-permute-done | bytes 131104 | tf_op jit(solution)/shard_map/ppermute | solution.py:25
  17.2 1.0 collective-permute-start.1
  18.3 2.5 %collective-permute-done.1 = bf16[256,256]{1,0:T(8,128)(2,1)S(1)} collective-permute-done((bf16[256,256]{1,0:T(8,128)(2,1)S(1)}, bf16[256,256]{1,0:T(8,128)(2,1)S(1)}, u32[]{:S(2)}, u32[]{:S(2)}) %collective-permute-start.1) | collective-permute-done | bytes 131104 | tf_op jit(solution)/shard_map/ppermute | solution.py:16
  20.8 1.5 collective-permute-start.2
  22.3 1.3 fusion.18
  23.6 6.7 %collective-permute-done.2 = bf16[512,256]{1,0:T(8,128)(2,1)S(1)} collective-permute-done((bf16[512,256]{1,0:T(8,128)(2,1)S(1)}, bf16[512,256]{1,0:T(8,128)(2,1)S(1)}, u32[]{:S(2)}, u32[]{:S(2)}) %collective-permute-start.2) | collective-permute-done | bytes 262176 | tf_op jit(solution)/shard_map/ppermute | solution.py:16
  30.6 0.5 broadcast.209
  31.1 0.7 reduce.6
  31.9 0.7 reduce.7
  33.4 13.9 %collective-permute-done.3 = bf16[1024,256]{1,0:T(8,128)(2,1)S(1)} collective-permute-done((bf16[1024,256]{1,0:T(8,128)(2,1)S(1)}, bf16[1024,256]{1,0:T(8,128)(2,1)S(1)}, u32[]{:S(2)}, u32[]{:S(2)}) %collective-permute-start.3) | collective-permute-done | bytes 524320 | tf_op jit(solution)/shard_map/ppermute | solution.py:16
  47.4 1.1 constant_dynamic-slice_fusion.7
  48.5 1.7 pad_maximum_fusion
  50.2 16.9 %while.50 = (s32[]{:T(128)}, bf16[2,16,256,256]{3,2,1,0:T(8,128)(2,1)}, s32[2,16]{1,0:T(2,128)S(1)}, bf16[4,256,256]{2,1,0:T(8,128)(2,1)S(1)}, s32[2,16]{1,0:T(2...) while((s32[]{:T(128)}, bf16[2,16,256,256]{3,2,1,0:T(8,128)(2,1)}, ...), condition=%wide.region_3.4_spmd, body=%wide.region_2.3_spmd.sunk | while | flops 540018816 | bytes 14689565 | solution.py:82
  50.2 2.0 %gather_fusion = bf16[16,256,256]{2,1,0:T(8,128)(2,1)} fusion(bf16[4,256,256]{2,1,0:T(8,128)(2,1)S(1)} %get-tuple-element.437, s32[1024]{0:T(1024)S(1)} %pad_clamp_fusion.12), kind=kCustom, calls=%fused_computation.clone.1 | custom fusion | bytes 4194368 | tf_op jit(solution)/shard_map/while/body/eval_jaxpr/gather | solution.py:71
  52.2 2.0 %gather_fusion.1 = bf16[16,256,256]{2,1,0:T(8,128)(2,1)} fusion(bf16[16,256,256]{2,1,0:T(8,128)(2,1)S(1)} %get-tuple-element.439, s32[1024]{0:T(1024)S(1)} %pad_clamp_fusion.13), kind=kCustom, calls=%fused_computation.1.clone.1 | custom fusion | bytes 4194368 | tf_op jit(solution)/shard_map/while/body/eval_jaxpr/gather | solution.py:72
  54.3 4.4 %bitcast_dynamic-update-slice_fusion.10 = bf16[2,16,256,256]{3,2,1,0:T(8,128)(2,1)} fusion(bf16[2,16,256,256]{3,2,1,0:T(8,128)(2,1)} %get-tuple-element.427, s32[]{:T(128)} %get-tuple-element.426, f32[16]{0:T(128)S(1)} %fusion.50, bf16[16,256,256]{2,1,0:T(8,128)(2,1)} %gather_fusion, bf16[16,256,256]{2,1,0:T(8,128)(2,1)} %gather_fusion.1), kind=kOutput, calls=%fused_computation.7.clone.1 | convolution fusion | flops 540016640 | bytes 6292032 | tf_op jit(solution)/shard_map/while/body/eval_jaxpr/pid,pjd->pij/dot_general | solution.py:73
  58.7 2.0 %gather_fusion = bf16[16,256,256]{2,1,0:T(8,128)(2,1)} fusion(bf16[4,256,256]{2,1,0:T(8,128)(2,1)S(1)} %get-tuple-element.437, s32[1024]{0:T(1024)S(1)} %pad_clamp_fusion.12), kind=kCustom, calls=%fused_computation.clone.1 | custom fusion | bytes 4194368 | tf_op jit(solution)/shard_map/while/body/eval_jaxpr/gather | solution.py:71
  60.7 2.0 %gather_fusion.1 = bf16[16,256,256]{2,1,0:T(8,128)(2,1)} fusion(bf16[16,256,256]{2,1,0:T(8,128)(2,1)S(1)} %get-tuple-element.439, s32[1024]{0:T(1024)S(1)} %pad_clamp_fusion.13), kind=kCustom, calls=%fused_computation.1.clone.1 | custom fusion | bytes 4194368 | tf_op jit(solution)/shard_map/while/body/eval_jaxpr/gather | solution.py:72
  62.7 4.3 %bitcast_dynamic-update-slice_fusion.10 = bf16[2,16,256,256]{3,2,1,0:T(8,128)(2,1)} fusion(bf16[2,16,256,256]{3,2,1,0:T(8,128)(2,1)} %get-tuple-element.427, s32[]{:T(128)} %get-tuple-element.426, f32[16]{0:T(128)S(1)} %fusion.50, bf16[16,256,256]{2,1,0:T(8,128)(2,1)} %gather_fusion, bf16[16,256,256]{2,1,0:T(8,128)(2,1)} %gather_fusion.1), kind=kOutput, calls=%fused_computation.7.clone.1 | convolution fusion | flops 540016640 | bytes 6292032 | tf_op jit(solution)/shard_map/while/body/eval_jaxpr/pid,pjd->pij/dot_general | solution.py:73
  67.1 10.6 %while.51 = (s32[]{:T(128)}, f32[2,16,256]{2,1,0:T(8,128)S(1)}, s32[2]{0:T(128)S(1)}, bf16[2,16,256,256]{3,2,1,0:T(8,128)(2,1)}, s32[2,16]{1,0:T(2,128)S(1)}, /*index=5*/s32[]{:T(128)}, f32[]{:T(128)}, s32[]{:T(128)}, s32[]{:T(128)}) while((s32[]{:T(128)}, f32[2,16,256]{2,1,0:T(8,128)S(1)}, s32[2]{0:T(128)S(1)}, ...), condition=%wide.region_6.7_spmd, body=%wide.region_4.6_spmd.sunk | while | flops 3142709 | bytes 2216347 | solution.py:101
  67.1 0.6 dynamic_slice.124
  69.6 0.6 gather_fusion.2
  70.2 2.2 %fusion.53 = f32[16,256]{1,0:T(8,128)S(1)} fusion(f32[16,256]{1,0:T(8,128)S(1)} %gather_fusion.2, bf16[2,16,256,256]{3,2,1,0:T(8,128)(2,1)} %get-tuple-element.463, s32[]{:T(128)S(6)} %select_n.117), kind=kLoop, calls=%fused_computation.22.clone.1 | loop fusion | flops 3141632 | bytes 2129924 | tf_op jit(solution)/shard_map/while/body/eval_jaxpr/reduce_sum | solution.py:97
  72.4 0.6 dynamic_slice.124
  74.9 0.6 gather_fusion.2
  75.5 2.2 %fusion.53 = f32[16,256]{1,0:T(8,128)S(1)} fusion(f32[16,256]{1,0:T(8,128)S(1)} %gather_fusion.2, bf16[2,16,256,256]{3,2,1,0:T(8,128)(2,1)} %get-tuple-element.463, s32[]{:T(128)S(6)} %select_n.117), kind=kLoop, calls=%fused_computation.22.clone.1 | loop fusion | flops 3141632 | bytes 2129924 | tf_op jit(solution)/shard_map/while/body/eval_jaxpr/reduce_sum | solution.py:97
  78.0 10.3 %while.52 = (s32[]{:T(128)}, f32[2,16,256]{2,1,0:T(8,128)S(1)}, s32[2]{0:T(128)S(1)}, bf16[2,16,256,256]{3,2,1,0:T(8,128)(2,1)}, s32[2,16]{1,0:T(2,128)S(1)}, /*...) while((s32[]{:T(128)}, f32[2,16,256]{2,1,0:T(8,128)S(1)}, s32[2]{0:T(128)S(1)}, ...), condition=%wide.region_9.10_spmd, body=%wide.region_7.9_spmd.sunk | while | flops 3142709 | bytes 2199959 | solution.py:112
  78.0 0.6 dynamic_slice.127
  80.6 0.6 gather_fusion.3
  81.2 1.9 %fusion.55 = f32[16,256]{1,0:T(8,128)S(1)} fusion(f32[16,256]{1,0:T(8,128)S(1)} %gather_fusion.3, bf16[2,16,256,256]{3,2,1,0:T(8,128)(2,1)} %get-tuple-element.490, s32[]{:T(128)S(6)} %select_n.119), kind=kLoop, calls=%fused_computation.30.clone.1 | loop fusion | flops 3141632 | bytes 2129924 | tf_op jit(solution)/shard_map/while/body/eval_jaxpr/reduce_sum | solution.py:108
  83.1 0.6 dynamic_slice.127
  85.7 0.6 gather_fusion.3
  86.3 1.9 %fusion.55 = f32[16,256]{1,0:T(8,128)S(1)} fusion(f32[16,256]{1,0:T(8,128)S(1)} %gather_fusion.3, bf16[2,16,256,256]{3,2,1,0:T(8,128)(2,1)} %get-tuple-element.490, s32[]{:T(128)S(6)} %select_n.119), kind=kLoop, calls=%fused_computation.30.clone.1 | loop fusion | flops 3141632 | bytes 2129924 | tf_op jit(solution)/shard_map/while/body/eval_jaxpr/reduce_sum | solution.py:108
  88.3 0.3 fusion.23
  88.6 0.6 dynamic-slice
  89.2 5.4 %collective-permute-done.4 = f32[8,256]{1,0:T(8,128)S(1)} collective-permute-done((f32[8,256]{1,0:T(8,128)S(1)}, f32[8,256]{1,0:T(8,128)S(1)}, u32[]{:S(2)}, u32[]{:S(2)}) %collective-permute-start.4) | collective-permute-done | bytes 8224 | tf_op jit(solution)/shard_map/ppermute | solution.py:25
  94.7 13.6 %all-reduce = f32[8,256]{1,0:T(8,128)S(1)} all-reduce(f32[8,256]{1,0:T(8,128)S(1)} %slice_add_fusion.1), channel_id=2, replica_groups=mesh['group'=4,'member'=8] {'member'}, use_global_device_ids=true, to_apply=%region_10.11.clone | all-reduce | flops 2048 | bytes 16384
  108.2 0.6 dynamic-slice_divide_fusion.1
  108.8 0.6 fusion.35
  109.5 1.8 %collective-permute-start.5 = (f32[1,256]{1,0:T(1,128)S(1)}, f32[1,256]{1,0:T(1,128)S(1)}, u32[]{:S(2)}, u32[]{:S(2)}) collective-permute-start(f32[1,256]{1,0:T(1,128)S(1)} %dynamic-slice_divide_fusion.1), channel_id=1, source_target_pairs={{0,24},{8,0},{16,8},{24,16},{1,25},{9,1},{17,9},{25,17},{2,26},{10... | collective-permute-start | bytes 3080 | tf_op jit(solution)/shard_map/ppermute | solution.py:25
  111.3 7.9 %all-gather = f32[8,1,256]{2,1,0:T(1,128)S(1)} all-gather(f32[1,1,256]{2,1,0:T(1,128)S(1)} %fusion.35), channel_id=1, replica_groups=mesh['group'=4,'member'=8] {'member'}, dimensions={0}, use_global_device_ids=true | all-gather | bytes 9216 | tf_op jit(solution)/shard_map/all_gather | solution.py:127
  119.1 9.0 %all-gather.1 = f32[8,1,256]{2,1,0:T(1,128)S(1)} all-gather(f32[1,1,256]{2,1,0:T(1,128)S(1)} %bitcast.167), channel_id=1, replica_groups=mesh['group'=4,'member'=8] {'member'}, dimensions={0}, use_global_device_ids=true | all-gather | bytes 9216 | tf_op jit(solution)/shard_map/all_gather | solution.py:128
  128.1 10.6 %while.53 = (s32[]{:T(128)}, f32[2,16,256]{2,1,0:T(8,128)S(1)}, s32[2]{0:T(128)S(1)}, bf16[2,16,256,256]{3,2,1,0:T(8,128)(2,1)}, s32[2,16]{1,0:T(2,128)S(1)}, /*...) while((s32[]{:T(128)}, f32[2,16,256]{2,1,0:T(8,128)S(1)}, s32[2]{0:T(128)S(1)}, ...), condition=%wide.region_13.14_spmd, body=%wide.region_11.13_spmd.sunk | while | flops 3142709 | bytes 2199959 | solution.py:101
  128.1 0.6 dynamic_slice.130
  130.6 0.6 gather_fusion.4
  131.2 2.2 %fusion.57 = f32[16,256]{1,0:T(8,128)S(1)} fusion(f32[16,256]{1,0:T(8,128)S(1)} %gather_fusion.4, bf16[2,16,256,256]{3,2,1,0:T(8,128)(2,1)} %get-tuple-element.517, s32[]{:T(128)S(6)} %select_n.121), kind=kLoop, calls=%fused_computation.38.clone.1 | loop fusion | flops 3141632 | bytes 2129924 | tf_op jit(solution)/shard_map/while/body/eval_jaxpr/reduce_sum | solution.py:97
  133.4 0.6 dynamic_slice.130
  135.9 0.6 gather_fusion.4
  136.5 2.2 %fusion.57 = f32[16,256]{1,0:T(8,128)S(1)} fusion(f32[16,256]{1,0:T(8,128)S(1)} %gather_fusion.4, bf16[2,16,256,256]{3,2,1,0:T(8,128)(2,1)} %get-tuple-element.517, s32[]{:T(128)S(6)} %select_n.121), kind=kLoop, calls=%fused_computation.38.clone.1 | loop fusion | flops 3141632 | bytes 2129924 | tf_op jit(solution)/shard_map/while/body/eval_jaxpr/reduce_sum | solution.py:97
  139.0 10.3 %while.54 = (s32[]{:T(128)}, f32[2,16,256]{2,1,0:T(8,128)S(1)}, s32[2]{0:T(128)S(1)}, bf16[2,16,256,256]{3,2,1,0:T(8,128)(2,1)}, s32[2,16]{1,0:T(2,128)S(1)}, /*...) while((s32[]{:T(128)}, f32[2,16,256]{2,1,0:T(8,128)S(1)}, s32[2]{0:T(128)S(1)}, ...), condition=%wide.region_16.17_spmd, body=%wide.region_14.16_spmd.sunk | while | flops 3142709 | bytes 2199959 | solution.py:112
  139.0 0.6 dynamic_slice.133
  141.6 0.6 gather_fusion.5
  142.2 1.9 %fusion.59 = f32[16,256]{1,0:T(8,128)S(1)} fusion(f32[16,256]{1,0:T(8,128)S(1)} %gather_fusion.5, bf16[2,16,256,256]{3,2,1,0:T(8,128)(2,1)} %get-tuple-element.544, s32[]{:T(128)S(6)} %select_n.123), kind=kLoop, calls=%fused_computation.46.clone.1 | loop fusion | flops 3141632 | bytes 2129924 | tf_op jit(solution)/shard_map/while/body/eval_jaxpr/reduce_sum | solution.py:108
  144.2 0.6 dynamic_slice.133
  146.7 0.6 gather_fusion.5
  147.3 1.9 %fusion.59 = f32[16,256]{1,0:T(8,128)S(1)} fusion(f32[16,256]{1,0:T(8,128)S(1)} %gather_fusion.5, bf16[2,16,256,256]{3,2,1,0:T(8,128)(2,1)} %get-tuple-element.544, s32[]{:T(128)S(6)} %select_n.123), kind=kLoop, calls=%fused_computation.46.clone.1 | loop fusion | flops 3141632 | bytes 2129924 | tf_op jit(solution)/shard_map/while/body/eval_jaxpr/reduce_sum | solution.py:108
  149.6 0.3 collective-permute-start.6
  149.9 0.6 copy.9
  150.5 4.6 %collective-permute-done.6 = f32[8,256]{1,0:T(8,128)S(1)} collective-permute-done((f32[8,256]{1,0:T(8,128)S(1)}, f32[8,256]{1,0:T(8,128)S(1)}, u32[]{:S(2)}, u32[]{:S(2)}) %collective-permute-start.6) | collective-permute-done | bytes 8224 | tf_op jit(solution)/shard_map/ppermute | solution.py:25
  155.1 12.3 %all-reduce.1 = f32[8,256]{1,0:T(8,128)S(1)} all-reduce(f32[8,256]{1,0:T(8,128)S(1)} %slice_add_fusion), channel_id=3, replica_groups=mesh['group'=4,'member'=8] {'member'}, use_global_device_ids=true, to_apply=%region_17.18.clone | all-reduce | flops 2048 | bytes 16384
  167.4 1.2 fusion.28
  (86 shorter events, 1.9 us)
Async XLA Ops:
  7.2 23.2 %copy-start = (bf16[1024,256]{1,0:T(8,128)(2,1)S(1)}, bf16[1024,256]{1,0:T(8,128)(2,1)}, u32[]{:S(2)}) copy-start(bf16[1024,256]{1,0:T(8,128)(2,1)} %param.15) | copy-start | bytes 1572868
  7.2 24.0 %copy-start.2 = (s32[1,32]{1,0:T(1,128)S(1)}, s32[1,32]{1,0:T(1,128)}, u32[]{:S(2)}) copy-start(s32[1,32]{1,0:T(1,128)} %param.17) | copy-start | bytes 388
  7.2 24.7 %copy-start.3 = (s32[1,32]{1,0:T(1,128)S(1)}, s32[1,32]{1,0:T(1,128)}, u32[]{:S(2)}) copy-start(s32[1,32]{1,0:T(1,128)} %param.18) | copy-start | bytes 388
  7.2 41.3 %all-gather.4.cloned.1.call-start = ((), (), s32[]{:S(2)}) async-start(), calls=%async_computation | async-start | bytes 1179648 | tf_op jit(solution)/shard_map/all_gather | solution.py:44
  9.3 8.9 %copy-start.1 = (bf16[256,256]{1,0:T(8,128)(2,1)}, bf16[256,256]{1,0:T(8,128)(2,1)S(1)}, u32[]{:S(2)}) copy-start(bf16[256,256]{1,0:T(8,128)(2,1)S(1)} %fusion.21) | copy-start | bytes 393220
  9.3 7.9 %collective-permute-start = (bf16[256,256]{1,0:T(8,128)(2,1)S(1)}, bf16[256,256]{1,0:T(8,128)(2,1)S(1)}, u32[]{:S(2)}, u32[]{:S(2)}) collective-permute-start(bf16[256,256]{1,0:T(8,128)(2,1)S(1)} %fusion.21), channel_id=1, source_target_pairs={{0,24},{8,0},{16,8},{24,16},{1,25},{9,1},{17,9},{25,17},{2,26},{10... | collective-permute-start | bytes 393224 | tf_op jit(solution)/shard_map/ppermute | solution.py:25
  17.2 3.6 %collective-permute-start.1 = (bf16[256,256]{1,0:T(8,128)(2,1)S(1)}, bf16[256,256]{1,0:T(8,128)(2,1)S(1)}, u32[]{:S(2)}, u32[]{:S(2)}) collective-permute-start(bf16[256,256]{1,0:T(8,128)(2,1)S(1)} %collective-permute-done), channel_id=1, source_target_pairs={{0,7},{1,0},{2,1},{3,2},{4,3},{5,4},{6,5},{7,6},{8,15},{9,8},{10,9... | collective-permute-start | bytes 393224 | tf_op jit(solution)/shard_map/ppermute | solution.py:16
  20.8 9.4 %collective-permute-start.2 = (bf16[512,256]{1,0:T(8,128)(2,1)S(1)}, bf16[512,256]{1,0:T(8,128)(2,1)S(1)}, u32[]{:S(2)}, u32[]{:S(2)}) collective-permute-start(bf16[512,256]{1,0:T(8,128)(2,1)S(1)} %pad_maximum_fusion.2), channel_id=1, source_target_pairs={{0,6},{1,7},{2,0},{3,1},{4,2},{5,3},{6,4},{7,5},{8,14},{9,15},{10,... | collective-permute-start | bytes 786440 | tf_op jit(solution)/shard_map/ppermute | solution.py:16
  30.3 17.0 %collective-permute-start.3 = (bf16[1024,256]{1,0:T(8,128)(2,1)S(1)}, bf16[1024,256]{1,0:T(8,128)(2,1)S(1)}, u32[]{:S(2)}, u32[]{:S(2)}) collective-permute-start(bf16[1024,256]{1,0:T(8,128)(2,1)S(1)} %pad_maximum_fusion.1), channel_id=1, source_target_pairs={{0,4},{1,5},{2,6},{3,7},{4,0},{5,1},{6,2},{7,3},{8,12},{9,13},{10,... | collective-permute-start | bytes 1572872 | tf_op jit(solution)/shard_map/ppermute | solution.py:16
  78.0 10.6 %copy-start.4 = (u32[32]{0:T(128)S(1)}, u32[32]{0:T(128)}, u32[]{:S(2)}) copy-start(u32[32]{0:T(128)} %constant.136) | copy-start | bytes 388
  88.5 6.1 %collective-permute-start.4 = (f32[8,256]{1,0:T(8,128)S(1)}, f32[8,256]{1,0:T(8,128)S(1)}, u32[]{:S(2)}, u32[]{:S(2)}) collective-permute-start(f32[8,256]{1,0:T(8,128)S(1)} %slice.29), channel_id=1, source_target_pairs={{0,8},{8,16},{16,24},{24,0},{1,9},{9,17},{17,25},{25,1},{2,10},{10... | collective-permute-start | bytes 24584 | tf_op jit(solution)/shard_map/ppermute | solution.py:25
  109.5 9.7 %collective-permute-start.5 = (f32[1,256]{1,0:T(1,128)S(1)}, f32[1,256]{1,0:T(1,128)S(1)}, u32[]{:S(2)}, u32[]{:S(2)}) collective-permute-start(f32[1,256]{1,0:T(1,128)S(1)} %dynamic-slice_divide_fusion.1), channel_id=1, source_target_pairs={{0,24},{8,0},{16,8},{24,16},{1,25},{9,1},{17,9},{25,17},{2,26},{10... | collective-permute-start | bytes 3080 | tf_op jit(solution)/shard_map/ppermute | solution.py:25
  149.6 5.5 %collective-permute-start.6 = (f32[8,256]{1,0:T(8,128)S(1)}, f32[8,256]{1,0:T(8,128)S(1)}, u32[]{:S(2)}, u32[]{:S(2)}) collective-permute-start(f32[8,256]{1,0:T(8,128)S(1)} %slice.31), channel_id=1, source_target_pairs={{0,8},{8,16},{16,24},{24,0},{1,9},{9,17},{17,25},{25,1},{2,10},{10... | collective-permute-start | bytes 24584 | tf_op jit(solution)/shard_map/ppermute | solution.py:25
Sparse Core Ops, SparseCore 0:
  18.4 29.6 all-gather.3
